TPU v7x, 128 devices: a whole 4x4x4 slice. The times are simulated.
128 devices in a mesh: dp: 16 (over z, y), mp: 8 (over x, core).
Axes of the slice: x: 4, y: 4, z: 4, core: 2. Of those that a mesh axis runs over, the one named last changes fastest.
Arguments:
- cotangent: bfloat16 [32768, 4096], P('dp'), may hold values from -64 to 64, as said below
- activation: bfloat16 [32768, 8192], P('dp', 'mp'), may hold values from -64 to 64, as said below
Outputs:
- update: bfloat16 [4096, 8192], P('dp', 'mp')
Inputs may be any that keep to these rules, and one draw needn't show every extreme that they name: `cotangent`: real-valued entries. `activation`: real-valued entries.
All inputs are finite; a program needn't handle non-finite values.
Results may differ from a plain program's by a relative error of at most 0.0054.
Values may be sent and summed in bfloat16 or wider, within the bound.
A program may use at most 256 MiB of HBM per device.

v0:
```python
import math

import jax
import jax.numpy as jnp
from jax import lax
from jax.sharding import PartitionSpec as P

N = 8192
ROWS = 4096


LINEAR_COEF = 3.4445
CUBIC_COEF = -4.775
QUINTIC_COEF = 2.0315
NORM_EPSILON = 1e-07
NORM_SHARE = 0.25
CONTRACT_FIRST = (((0,), (0,)), ((), ()))
CONTRACT_LAST = (((1,), (1,)), ((), ()))


def local(cotangent, activation):
    section = cotangent
    gradient = lax.psum_scatter(
        lax.dot_general(section, activation, CONTRACT_FIRST, preferred_element_type=jnp.float32),
        "dp",
        scatter_dimension=0,
        tiled=True,
    )
    sum_squares = lax.psum(jnp.sum(gradient * gradient), ("dp", "mp"))
    factor = NORM_SHARE * math.sqrt(ROWS) / (jnp.sqrt(sum_squares) + NORM_EPSILON)
    normalized = (gradient * factor).astype(jnp.bfloat16)
    weight_column = lax.all_gather(normalized, "dp", axis=0, tiled=True)
    section = weight_column
    gram_tile = lax.psum_scatter(
        lax.dot_general(section, normalized, CONTRACT_LAST, preferred_element_type=jnp.float32),
        "mp",
        scatter_dimension=0,
        tiled=True,
    ).T.astype(jnp.bfloat16)
    row_panel = lax.all_gather(gram_tile, "mp", axis=1, tiled=True)
    section = row_panel
    square_tile = jnp.dot(
        section,
        lax.all_gather(gram_tile, "dp", axis=0, tiled=True),
        preferred_element_type=jnp.float32,
    )
    polynomial = (CUBIC_COEF * gram_tile.astype(jnp.float32) + QUINTIC_COEF * square_tile).astype(
        jnp.bfloat16
    )
    section = weight_column
    product_tile = jnp.dot(
        lax.all_gather(polynomial, "mp", axis=1, tiled=True),
        section,
        preferred_element_type=jnp.float32,
    )
    rescale = math.sqrt(N)
    return (rescale * (LINEAR_COEF * normalized.astype(jnp.float32) + product_tile)).astype(
        jnp.bfloat16
    )


def solution(mesh):
    return jax.shard_map(
        local,
        mesh=mesh,
        in_specs=(P("dp", None), P("dp", "mp")),
        out_specs=P("dp", "mp"),
        check_vma=False,
    )
```

profile of v0, /device:TPU:6, one launch (start us, length us, event | category | flops | bytes accessed | tf_op | source)
XLA Modules:
  0.0 455.0 jit_solution(6413023268243869418)
XLA Ops:
  6.5 0.0 reduce-scatter.3.cloned.1.call-start
  6.5 23.7 %fusion.4 = f32[4096,1024]{1,0:T(8,128)} fusion(bf16[2048,4096]{1,0:T(8,128)(2,1)} %param.2, bf16[2048,1024]{1,0:T(8,128)(2,1)} %param.3), kind=kOutput, calls=%fused_computation.9 | convolution fusion | flops 17179869184 | bytes 37748736 | tf_op jit(solution)/shard_map/dot_general | solution.py:24
  30.3 0.0 reduce-scatter.3.cloned.1.call-update
  30.3 0.0 all-gather.5.cloned.1.call-start
  30.3 113.1 %reduce-scatter.3.cloned.1.call-done = f32[256,1024]{1,0:T(8,128)} async-done(((f32[4096,1024]{1,0:T(8,128)}), f32[256,1024]{1,0:T(8,128)}) %reduce-scatter.3.cloned.1.call-update) | async-done | bytes 1048592 | tf_op jit(solution)/shard_map/reduce_scatter | solution.py:23
  143.5 2.1 multiply_reduce_fusion
  145.6 64.3 %psum.7 = f32[]{:T(128)} all-reduce(f32[]{:T(128)} %multiply_reduce_fusion), channel_id=1, replica_groups=mesh['dp'=16,'mp'=8] {'dp','mp'}, use_global_device_ids=true, to_apply=%region_2.0 | all-reduce | flops 1 | bytes 8 | tf_op jit(solution)/shard_map/psum | solution.py:29
  210.6 2.1 multiply_convert_fusion
  212.7 0.0 all-gather.5.cloned.1.call-update
  212.7 0.0 reduce-scatter.5.cloned.1.call-start
  212.8 68.4 %all-gather.5.cloned.1.call-done = bf16[4096,1024]{1,0:T(8,128)(2,1)} async-done(((bf16[256,1024]{1,0:T(8,128)(2,1)}), bf16[4096,1024]{1,0:T(8,128)(2,1)}) %all-gather.5.cloned.1.call-update) | async-done | bytes 8388624 | tf_op jit(solution)/shard_map/all_gather | solution.py:32
  281.1 7.8 %fusion.5 = f32[4096,256]{1,0:T(8,128)} fusion(bf16[4096,1024]{1,0:T(8,128)(2,1)} %all-gather.5.cloned.1.call-done, bf16[256,1024]{1,0:T(8,128)(2,1)} %multiply_convert_fusion), kind=kOutput, calls=%fused_computation.10 | convolution fusion | flops 2147483648 | bytes 13107200 | tf_op jit(solution)/shard_map/dot_general | solution.py:35
  288.9 0.0 reduce-scatter.5.cloned.1.call-update
  288.9 0.0 all-gather.7.cloned.1.call-start
  289.0 34.0 %reduce-scatter.5.cloned.1.call-done = f32[512,256]{1,0:T(8,128)} async-done(((f32[4096,256]{1,0:T(8,128)}), f32[512,256]{1,0:T(8,128)}) %reduce-scatter.5.cloned.1.call-update) | async-done | bytes 524304 | tf_op jit(solution)/shard_map/reduce_scatter | solution.py:34
  323.0 1.8 convert_bitcast_fusion
  324.8 0.0 all-gather.7.cloned.1.call-update
  324.8 0.0 all-gather.9.cloned.1.call-start
  324.9 0.5 all-gather.9.cloned.1.call-update
  325.4 0.0 copy-start
  325.4 0.0 all-gather.11.cloned.1.call-start
  325.5 26.2 %all-gather.7.cloned.1.call-done = bf16[256,4096]{0,1:T(8,128)(2,1)} async-done(((bf16[256,512]{0,1:T(8,128)(2,1)}), bf16[256,4096]{0,1:T(8,128)(2,1)}) %all-gather.7.cloned.1.call-update) | async-done | bytes 2097168 | tf_op jit(solution)/shard_map/all_gather | solution.py:40
  351.6 61.0 %all-gather.9.cloned.1.call-done = bf16[4096,512]{0,1:T(8,128)(2,1)} async-done(((bf16[256,512]{0,1:T(8,128)(2,1)}), bf16[4096,512]{0,1:T(8,128)(2,1)}) %all-gather.9.cloned.1.call-update) | async-done | bytes 4194320 | tf_op jit(solution)/shard_map/all_gather | solution.py:44
  412.6 4.8 %fusion.3 = bf16[256,512]{0,1:T(8,128)(2,1)} fusion(bf16[4096,512]{0,1:T(8,128)(2,1)} %all-gather.9.cloned.1.call-done, bf16[256,4096]{0,1:T(8,128)(2,1)} %all-gather.7.cloned.1.call-done, bf16[256,512]{0,1:T(8,128)(2,1)} %convert_bitcast_fusion), kind=kOutput, calls=%fused_computation.5 | convolution fusion | flops 1074397184 | bytes 6815744 | tf_op jit(solution)/shard_map/dot_general | solution.py:42
  417.4 0.0 all-gather.11.cloned.1.call-update
  417.4 23.6 %all-gather.11.cloned.1.call-done = bf16[256,4096]{0,1:T(8,128)(2,1)} async-done(((bf16[256,512]{0,1:T(8,128)(2,1)}), bf16[256,4096]{0,1:T(8,128)(2,1)}) %all-gather.11.cloned.1.call-update) | async-done | bytes 2097168 | tf_op jit(solution)/shard_map/all_gather | solution.py:52
  441.0 0.0 copy-done
  441.0 7.2 %fusion.1 = bf16[256,1024]{1,0:T(8,128)(2,1)} fusion(bf16[256,4096]{0,1:T(8,128)(2,1)} %all-gather.11.cloned.1.call-done, bf16[4096,1024]{1,0:T(8,128)(2,1)} %all-gather.5.cloned.1.call-done, bf16[256,1024]{1,0:T(8,128)(2,1)S(1)} %copy-done), kind=kOutput, calls=%fused_computation.2 | convolution fusion | flops 2148794368 | bytes 11534336 | tf_op jit(solution)/shard_map/dot_general | solution.py:51
Async XLA Ops:
  6.5 136.9 %reduce-scatter.3.cloned.1.call-start = ((), (), s32[]{:S(2)}) async-start(), calls=%async_computation.2 | async-start | bytes 17825792 | tf_op jit(solution)/shard_map/reduce_scatter | solution.py:23
  30.3 250.8 %all-gather.5.cloned.1.call-start = ((), (), s32[]{:S(2)}) async-start(), calls=%async_computation.3 | async-start | bytes 8912896 | tf_op jit(solution)/shard_map/all_gather | solution.py:32
  212.7 110.3 %reduce-scatter.5.cloned.1.call-start = ((), (), s32[]{:S(2)}) async-start(), calls=%async_computation.4 | async-start | bytes 4718592 | tf_op jit(solution)/shard_map/reduce_scatter | solution.py:34
  288.9 62.7 %all-gather.7.cloned.1.call-start = ((), (), s32[]{:S(2)}) async-start(), calls=%async_computation.5 | async-start | bytes 2359296 | tf_op jit(solution)/shard_map/all_gather | solution.py:40
  324.8 87.8 %all-gather.9.cloned.1.call-start = ((), (), s32[]{:S(2)}) async-start(), calls=%async_computation.6 | async-start | bytes 4456448 | tf_op jit(solution)/shard_map/all_gather | solution.py:44
  325.4 115.6 %copy-start = (bf16[256,1024]{1,0:T(8,128)(2,1)S(1)}, bf16[256,1024]{1,0:T(8,128)(2,1)}, u32[]{:S(2)}) copy-start(bf16[256,1024]{1,0:T(8,128)(2,1)} %multiply_convert_fusion) | copy-start | bytes 1572868
  325.4 115.6 %all-gather.11.cloned.1.call-start = ((), (), s32[]{:S(2)}) async-start(), calls=%async_computation.7 | async-start | bytes 2359296 | tf_op jit(solution)/shard_map/all_gather | solution.py:52
Sparse Core Ops, SparseCore 0:
  30.4 113.0 reduce-scatter.2
  212.8 68.2 all-gather.4
  289.0 33.9 reduce-scatter.4
  324.9 26.6 all-gather.6
  353.6 58.9 all-gather.8
  417.6 23.4 all-gather.10
where the time goes:
time: 458 us; the launch traced here: 455 us
  waiting for transfers between devices  327 us (71%)
  blocking collectives  64.3 us (14%)
  matrix products  43.5 us (9%)
  between operations  14.2 us (3%)
  other arithmetic  6 us (1%)
    reduce_scatter x1, waiting for transfers between devices, local(): lax.psum_scatter(lax.dot_general(section, activation, CONTRACT_FIRST, pre...  113 us
    all_gather x1, waiting for transfers between devices, local(): weight_column = lax.all_gather(normalized, 'dp', axis=0, tiled=True)  68.4 us
    psum x1, blocking collectives, local(): sum_squares = lax.psum(jnp.sum(gradient * gradient), ('dp', 'mp'))  64.3 us
    all_gather x1, waiting for transfers between devices, local(): lax.all_gather(gram_tile, 'dp', axis=0, tiled=True)  61 us
    reduce_scatter x1, waiting for transfers between devices, local(): lax.psum_scatter(lax.dot_general(section, normalized, CONTRACT_LAST, pref...  34 us
    all_gather x1, waiting for transfers between devices, local(): row_panel = lax.all_gather(gram_tile, 'mp', axis=1, tiled=True)  26.2 us
    dot_general x1, matrix products, local(): lax.dot_general(section, activation, CONTRACT_FIRST, preferred_element_ty...  23.7 us
    all_gather x1, waiting for transfers between devices, local(): lax.all_gather(polynomial, 'mp', axis=1, tiled=True)  23.6 us
  transfers between devices with their start and end apart: 6, of which 6 were waited for; matrix products, arithmetic and copies ran while one was open for 0% of the time, Pallas kernels for 0%

commit v1 on v0

v1 whole, which is shorter than its diff:
```python
import math

import jax
import jax.numpy as jnp
from jax import lax
from jax.experimental import pallas as pl
from jax.experimental.pallas import tpu as pltpu
from jax.sharding import PartitionSpec as P

N = 8192
ROWS = 4096

LINEAR_COEF = 3.4445
CUBIC_COEF = -4.775
QUINTIC_COEF = 2.0315
NORM_EPSILON = 1e-07
NORM_SHARE = 0.25

BF = jnp.bfloat16
F32 = jnp.float32
NN = (((1,), (0,)), ((), ()))
NT = (((1,), (1,)), ((), ()))
SHIFT = (0, 1, 3, 2)
PLUS, MINUS = 0, 1


def dot(a, b, dims=NN):
    return lax.dot_general(a, b, dims, preferred_element_type=F32)


def kernel(
    c_ref, a_ref, out_ref,
    a_t, a_in, c_in, a_sem, c_sem,
    far_out, far_in, near_out, near_in, via_out, via_in, via_sum, own_sum, g_send, g_recv,
    rs_far_out, rs_far_in, rs_near_out, rs_near_in, rs_via_out, rs_via_in, rs_via, rs_own, rs_send, rs_recv,
    grad, z_group, y_group, ag_send, ag_recv,
    tile, half_out, half_in, pair_send, pair_recv,
    x_far_out, x_far_in, x_near_out, x_near_in, x_via_out, x_via_in, x_send, x_recv,
    gram, gx_send, gx_recv, gp_send, gp_recv,
    values, sq, sq_send, sq_recv,
):
    dp, mp = lax.axis_index("dp"), lax.axis_index("mp")
    z, y = dp // 4, lax.rem(dp, 4)
    x, core = mp // 2, lax.rem(mp, 2)

    def at(axis, step):
        if axis == "z":
            return (lax.rem(z + step, 4) * 4 + y, mp)
        if axis == "y":
            return (z * 4 + lax.rem(y + step, 4), mp)
        if axis == "x":
            return (dp, lax.rem(x + step, 4) * 2 + core)
        return (dp, x * 2 + 1 - core)

    STEP = (1, 3)
    sent = []

    def copy(src, dst, send, recv, axis, direction):
        return pltpu.make_async_remote_copy(
            src_ref=src, dst_ref=dst, send_sem=send, recv_sem=recv,
            device_id=at(axis, STEP[direction]), device_id_type=pl.DeviceIdType.MESH,
        )

    def send(*args):
        c = copy(*args)
        c.start()
        sent.append(c)
        return c

    def load_a(q):
        return pltpu.make_async_copy(a_ref.at[:, pl.ds(q * 256, 256)], a_in.at[q % 2], a_sem.at[q % 2])

    def pick(k):
        return jnp.where(k == 0, 2, jnp.where(k == 1, 1, jnp.where(k == 2, 3, 0)))

    def block(u):
        first = u < 8
        last = u >= 24
        v = jnp.where(first, u, jnp.where(last, u - 24, u - 8))
        pairs = first | last
        k = jnp.where(pairs, v // 2, v // 4)
        h = jnp.where(pairs, lax.rem(v, 2), lax.rem(v // 2, 2))
        d = lax.rem(v, 2)
        step = jnp.where(first, 2, jnp.where(last, 0, 1 + 2 * d))
        one = jnp.where(h == 0, z, y)
        two = jnp.where(h == 0, y, z)
        one = lax.rem(one + step, 4)
        two = lax.rem(two + pick(k), 4)
        return jnp.where(h == 0, one * 4 + two, two * 4 + one)

    def load_c(u):
        slot = lax.rem(u, 4)
        col = pl.multiple_of(block(u) * 256, 256)
        return pltpu.make_async_copy(c_ref.at[:, pl.ds(col, 256)], c_in.at[slot], c_sem.at[slot])

    load_a(0).start()
    load_a(1).start()
    for u in range(3):
        load_c(jnp.int32(u)).start()

    barrier = pltpu.get_barrier_semaphore()
    for axis in ("z", "y", "x"):
        for step in (1, 2, 3):
            pl.semaphore_signal(barrier, inc=1, device_id=at(axis, step), device_id_type=pl.DeviceIdType.MESH)
    pl.semaphore_signal(barrier, inc=1, device_id=at("core", 0), device_id_type=pl.DeviceIdType.MESH)

    for q in range(4):
        load_a(q).wait()
        a_t[pl.ds(q * 256, 256), :] = a_in[q % 2].T
        if q < 2:
            load_a(q + 2).start()
    pl.semaphore_wait(barrier, 10)

    AXIS1 = ("z", "y")
    AXIS2 = ("y", "z")

    def unit(h, u):
        @pl.when(u + 3 < 32)
        def _():
            load_c(u + 3).start()

        load_c(u).wait()
        return dot(a_t[pl.ds(h * 512, 512), :], c_in[lax.rem(u, 4)])

    def far_copy(h, d, k):
        return copy(far_out.at[h, k, pl.ds(d * 256, 256)], far_in.at[h, d, k],
                    g_send.at[0, h, d, k], g_recv.at[0, h, d, k], AXIS1[h], d)

    def near_copy(h, d, k):
        return copy(near_out.at[h, d, k], near_in.at[h, d, k],
                    g_send.at[1, h, d, k], g_recv.at[1, h, d, k], AXIS1[h], d)

    def via_copy(h, d, k):
        return copy(via_out.at[h, d, k], via_in.at[h, d, k],
                    g_send.at[2, h, d, k], g_recv.at[2, h, d, k], AXIS1[h], d)

    def far_body(k, carry):
        for h in range(2):
            far_out[h, k] = unit(h, 2 * k + h).astype(BF)
            for d in range(2):
                far_copy(h, d, k).start()
        return carry

    def near_body(k, carry):
        for h in range(2):
            for d in range(2):
                r = unit(h, 8 + 4 * k + 2 * h + d)
                direct, relayed = 1 - d, d
                near_out[h, d, k] = r[direct * 256:direct * 256 + 256].astype(BF)
                via_sum[h, d, k] = r[relayed * 256:relayed * 256 + 256]
                near_copy(h, d, k).start()
        return carry

    def via_body(k, carry):
        for h in range(2):
            for d in range(2):
                far_copy(h, d, k).wait_recv()
                via_out[h, d, k] = (via_sum[h, d, k] + far_in[h, d, k].astype(F32)).astype(BF)
                via_copy(h, d, k).start()
        return carry

    def own_body(k, carry):
        for h in range(2):
            own_sum[h, k] = unit(h, 24 + 2 * k + h)
        return carry

    lax.fori_loop(0, 4, far_body, 0)
    lax.fori_loop(0, 4, near_body, 0)
    lax.fori_loop(0, 4, via_body, 0)
    lax.fori_loop(0, 4, own_body, 0)

    def first_sum(h, k):
        for d in range(2):
            near_copy(h, d, k).wait_recv()
            via_copy(h, d, k).wait_recv()
        top = own_sum[h, k, 0:256] + via_in[h, 0, k].astype(F32) + near_in[h, 1, k].astype(F32)
        low = own_sum[h, k, 256:512] + near_in[h, 0, k].astype(F32) + via_in[h, 1, k].astype(F32)
        return top, low

    def rs_copy(n, h, kind, d, axis):
        src, dst = (
            (rs_far_out.at[n, h, pl.ds(d * 256, 256)], rs_far_in.at[n, h, d]),
            (rs_near_out.at[n, h, d], rs_near_in.at[n, h, d]),
            (rs_via_out.at[n, h, d], rs_via_in.at[n, h, d]),
        )[kind]
        return src, dst, rs_send.at[n, h, kind, d], rs_recv.at[n, h, kind, d], axis, d

    def rs_put(n, h, axis, slot, top, low):
        if slot == 3:
            rs_far_out[n, h, 0:256] = top.astype(BF)
            rs_far_out[n, h, 256:512] = low.astype(BF)
            for d in range(2):
                send(*rs_copy(n, h, 0, d, axis))
        elif slot == 1:
            rs_near_out[n, h, 0] = low.astype(BF)
            send(*rs_copy(n, h, 1, 0, axis))
            rs_via[h, 0] = top
        elif slot == 2:
            rs_near_out[n, h, 1] = top.astype(BF)
            send(*rs_copy(n, h, 1, 1, axis))
            rs_via[h, 1] = low
        else:
            rs_own[h, 0:256] = top
            rs_own[h, 256:512] = low

    def rs_relay(n, h, axis):
        for d in range(2):
            copy(*rs_copy(n, h, 0, d, axis)).wait_recv()
            rs_via_out[n, h, d] = (rs_via[h, d] + rs_far_in[n, h, d].astype(F32)).astype(BF)
            send(*rs_copy(n, h, 2, d, axis))

    def rs_finish(n, h, axis):
        for kind in (1, 2):
            for d in range(2):
                copy(*rs_copy(n, h, kind, d, axis)).wait_recv()
        top = rs_own[h, 0:256] + rs_via_in[n, h, 0].astype(F32) + rs_near_in[n, h, 1].astype(F32)
        low = rs_own[h, 256:512] + rs_near_in[n, h, 0].astype(F32) + rs_via_in[n, h, 1].astype(F32)
        return top, low

    def ag_copy(n, buf, rows, kind, d, axis):
        part = d if kind in (0, 2) else 1 - d
        there = (2, 1)[d]
        here, target = (0, there) if kind < 2 else (there, 3)
        r = pl.ds(part * rows, rows)
        return (buf.at[r, pl.ds(here * 256, 256)], buf.at[r, pl.ds(target * 256, 256)],
                ag_send.at[n, kind, d], ag_recv.at[n, kind, d], axis, d)

    def ag_own(n, buf, rows, axis, part):
        for d in range(2):
            send(*ag_copy(n, buf, rows, 0 if d == part else 1, d, axis))

    def ag_relay(n, buf, rows, axis):
        for d in range(2):
            copy(*ag_copy(n, buf, rows, 0, d, axis)).wait_recv()
            send(*ag_copy(n, buf, rows, 2, d, axis))

    def ag_near(n, buf, rows, axis):
        for d in range(2):
            copy(*ag_copy(n, buf, rows, 1, d, axis)).wait_recv()

    def ag_far(n, buf, rows, axis):
        for d in range(2):
            copy(*ag_copy(n, buf, rows, 2, d, axis)).wait_recv()

    for k, slot in ((0, 3), (1, 1), (2, 2)):
        for h in range(2):
            top, low = first_sum(h, k)
            rs_put(0, h, AXIS2[h], slot, top, low)
    for h in range(2):
        rs_relay(0, h, AXIS2[h])
    for h in range(2):
        top, low = first_sum(h, 3)
        rs_put(0, h, AXIS2[h], 0, top, low)

    squares = jnp.zeros((1, 256), F32)
    for h in range(2):
        top, low = rs_finish(0, h, AXIS2[h])
        grad[h, 0:256] = top
        grad[h, 256:512] = low
        for part, value in ((0, top), (1, low)):
            r = pl.ds(h * 512 + part * 256, 256)
            z_group[r, 0:256] = value.astype(BF)
            y_group[r, 0:256] = value.astype(BF)
            squares += jnp.sum(value * value, axis=0, keepdims=True)
        ag_own(0, z_group, 512, "y", h)
        ag_own(1, y_group, 512, "z", h)

    def sq_copies(n, axis):
        if axis == "core":
            steps = (1,)
        else:
            steps = (1, 2, 3)
        return [
            pltpu.make_async_remote_copy(
                src_ref=sq.at[n, 0], dst_ref=sq.at[n, step],
                send_sem=sq_send.at[n, step], recv_sem=sq_recv.at[n, step],
                device_id=at(axis, step), device_id_type=pl.DeviceIdType.MESH,
            )
            for step in steps
        ]

    def sq_start(n, axis, value):
        sq[n, 0] = jnp.broadcast_to(value, (8, 256))
        for c in sq_copies(n, axis):
            c.start()
            sent.append(c)

    def sq_total(n, axis):
        total = sq[n, 0]
        for step, c in enumerate(sq_copies(n, axis)):
            c.wait_recv()
            total += sq[n, step + 1]
        return total

    sq_start(0, "z", squares)

    ag_relay(0, z_group, 512, "y")
    ag_relay(1, y_group, 512, "z")
    ag_near(0, z_group, 512, "y")
    ag_near(1, y_group, 512, "z")

    def turn(slot):
        a_t[pl.ds(slot * 256, 256), 0:1024] = z_group[:, slot * 256:slot * 256 + 256].T

    for slot in range(3):
        turn(slot)
    sq_start(1, "y", sq_total(0, "z"))
    ag_far(0, z_group, 512, "y")
    ag_far(1, y_group, 512, "z")
    turn(3)

    mine = pl.multiple_of(core * 512, 512)
    other = pl.multiple_of((1 - core) * 512, 512)

    def half_copy(step):
        r = pl.ds(pl.multiple_of(lax.rem(x + step, 4) * 128, 128), 128)
        return half_out.at[r], half_in.at[r], pair_send.at[step], pair_recv.at[step], "core", 0

    def other_body(i, carry):
        cols = pl.ds(pl.multiple_of(i * 256, 256), 256)
        half_out[:, cols] = dot(a_t[pl.ds(other, 512), 0:1024], y_group[:, cols]).astype(BF)
        return carry

    def mine_body(i, carry):
        cols = pl.ds(pl.multiple_of(i * 256, 256), 256)
        tile[:, cols] = dot(a_t[pl.ds(mine, 512), 0:1024], y_group[:, cols])
        return carry

    lax.fori_loop(0, 4, other_body, 0)
    for step in (2, 1, 3, 0):
        send(*half_copy(step))
    lax.fori_loop(0, 4, mine_body, 0)
    sq_start(2, "x", sq_total(1, "y"))

    def pair_sum(step):
        copy(*half_copy(step)).wait_recv()
        r = pl.ds(pl.multiple_of(lax.rem(x + step, 4) * 128, 128), 128)
        return tile[r, :] + half_in[r, :].astype(F32)

    def x_copy(kind, d):
        src, dst = (
            (x_far_out.at[d], x_far_in.at[d]),
            (x_near_out.at[d], x_near_in.at[d]),
            (x_via_out.at[d], x_via_in.at[d]),
        )[kind]
        return src, dst, x_send.at[kind, d], x_recv.at[kind, d], "x", d

    s = pair_sum(2)
    for d in range(2):
        x_far_out[d] = s[:, d * 512:d * 512 + 512].astype(BF)
        send(*x_copy(0, d))
    relayed = []
    for d in range(2):
        s = pair_sum(STEP[d])
        x_near_out[d] = s[:, (1 - d) * 512:(1 - d) * 512 + 512].astype(BF)
        send(*x_copy(1, d))
        r = pl.ds(pl.multiple_of(lax.rem(x + STEP[d], 4) * 128, 128), 128)
        tile[r, d * 512:d * 512 + 512] = s[:, d * 512:d * 512 + 512]
    s = pair_sum(0)
    here = pl.ds(pl.multiple_of(x * 128, 128), 128)
    tile[here, :] = s
    for d in range(2):
        copy(*x_copy(0, d)).wait_recv()
        r = pl.ds(pl.multiple_of(lax.rem(x + STEP[d], 4) * 128, 128), 128)
        x_via_out[d] = (tile[r, d * 512:d * 512 + 512] + x_far_in[d].astype(F32)).astype(BF)
        send(*x_copy(2, d))
    for kind in (1, 2):
        for d in range(2):
            copy(*x_copy(kind, d)).wait_recv()

    def chunk(step, part):
        r = pl.ds(pl.multiple_of(core * 512 + lax.rem(x + step, 4) * 128, 128), 128)
        return gram.at[r, pl.ds(part * 512, 512)]

    chunk(0, 0)[...] = (
        tile[here, 0:512] + x_via_in[0].astype(F32) + x_near_in[1].astype(F32)
    ).astype(BF)
    chunk(0, 1)[...] = (
        tile[here, 512:1024] + x_near_in[0].astype(F32) + x_via_in[1].astype(F32)
    ).astype(BF)

    def gx_copy(kind, d):
        part = d if kind in (0, 2) else 1 - d
        step = 0 if kind < 2 else STEP[1 - d]
        return chunk(step, part), chunk(step, part), gx_send.at[kind, d], gx_recv.at[kind, d], "x", d

    def gx_arrived(kind, d):
        part = d if kind in (0, 2) else 1 - d
        step = STEP[1 - d] if kind < 2 else 2
        ref = chunk(step, part)
        copy(ref, ref, gx_send.at[kind, d], gx_recv.at[kind, d], "x", d).wait_recv()
        return step, part

    def gp_copy(step, part):
        ref = chunk(step, part)
        return ref, ref, gp_send.at[step, part], gp_recv.at[step, part], "core", 0

    for kind in (0, 1):
        for d in range(2):
            send(*gx_copy(kind, d))
    for part in range(2):
        send(*gp_copy(0, part))
    sq_start(3, "core", sq_total(2, "x"))
    arrived = []
    for d in range(2):
        arrived.append(gx_arrived(0, d))
        send(*gx_copy(2, d))
    for d in range(2):
        send(*gp_copy(*arrived[d]))
    for kind in (1, 2):
        for d in range(2):
            send(*gp_copy(*gx_arrived(kind, d)))
    for step in range(4):
        for part in range(2):
            r = pl.ds(pl.multiple_of((1 - core) * 512 + lax.rem(x + step, 4) * 128, 128), 128)
            ref = gram.at[r, pl.ds(part * 512, 512)]
            copy(ref, ref, gp_send.at[step, part], gp_recv.at[step, part], "core", 0).wait_recv()

    total = jnp.sum(sq_total(3, "core")[0:1, :], axis=1, keepdims=True)
    factor = NORM_SHARE * math.sqrt(ROWS) / (jnp.sqrt(total) + NORM_EPSILON)

    def down(lhs, slot):
        return dot(lhs, gram[:, slot * 256:slot * 256 + 256])

    def across(lhs, slot):
        return dot(lhs, gram[slot * 256:slot * 256 + 256, :], NT)

    for slot in (3, 1, 2, 0):
        w = down(z_group[0:512, :], slot)
        rs_put(1, 0, "z", slot, w[0:256], w[256:512])
        w = across(y_group[512:1024, :], slot)
        rs_put(1, 1, "y", slot, w[0:256], w[256:512])
    for h in range(2):
        rs_relay(1, h, AXIS1[h])
    for h in range(2):
        for part, w in enumerate(rs_finish(1, h, AXIS1[h])):
            r = pl.ds(part * 256, 256)
            v = CUBIC_COEF * grad[h, r] + (QUINTIC_COEF * factor * factor) * w
            values[h, r, 0:256] = v.astype(BF)
            ag_own(2 + h, values.at[h], 256, AXIS1[h], part)
    for h in range(2):
        ag_relay(2 + h, values.at[h], 256, AXIS1[h])
    for h in range(2):
        ag_near(2 + h, values.at[h], 256, AXIS1[h])
        ag_far(2 + h, values.at[h], 256, AXIS1[h])
    for slot in (3, 1, 2, 0):
        m = across(values[0], slot)
        rs_put(2, 0, "y", slot, m[0:256], m[256:512])
        m = down(values[1], slot)
        rs_put(2, 1, "z", slot, m[0:256], m[256:512])
    for h in range(2):
        rs_relay(2, h, AXIS2[h])
    scale = math.sqrt(N) * factor
    for h in range(2):
        for part, m in enumerate(rs_finish(2, h, AXIS2[h])):
            r = pl.ds(part * 256, 256)
            o = scale * (LINEAR_COEF * grad[h, r] + (factor * factor) * m)
            out_ref[:, h * 512 + part * 256:h * 512 + part * 256 + 256] = o.T.astype(BF)

    def drain(k, carry):
        for h in range(2):
            for d in range(2):
                far_copy(h, d, k).wait_send()
                near_copy(h, d, k).wait_send()
                via_copy(h, d, k).wait_send()
        return carry

    lax.fori_loop(0, 4, drain, 0)
    for c in sent:
        c.wait_send()


def local(cotangent, activation):
    dma = pltpu.SemaphoreType.DMA
    vm = pltpu.VMEM
    piece = (256, 256)
    return pl.pallas_call(
        kernel,
        out_shape=jax.ShapeDtypeStruct((256, 1024), BF),
        in_specs=[pl.BlockSpec(memory_space=pl.ANY)] * 2,
        out_specs=pl.BlockSpec(memory_space=pltpu.VMEM),
        scratch_shapes=[
            vm((1024, 2048), BF), vm((2, 2048, 256), BF), vm((4, 2048, 256), BF), dma((2,)), dma((4,)),
            vm((2, 4, 512, 256), BF), vm((2, 2, 4) + piece, BF),
            vm((2, 2, 4) + piece, BF), vm((2, 2, 4) + piece, BF),
            vm((2, 2, 4) + piece, BF), vm((2, 2, 4) + piece, BF),
            vm((2, 2, 4) + piece, F32), vm((2, 4, 512, 256), F32),
            dma((3, 2, 2, 4)), dma((3, 2, 2, 4)),
            vm((3, 2, 512, 256), BF), vm((3, 2, 2) + piece, BF),
            vm((3, 2, 2) + piece, BF), vm((3, 2, 2) + piece, BF),
            vm((3, 2, 2) + piece, BF), vm((3, 2, 2) + piece, BF),
            vm((2, 2) + piece, F32), vm((2, 512, 256), F32),
            dma((3, 2, 3, 2)), dma((3, 2, 3, 2)),
            vm((2, 512, 256), F32), vm((1024, 1024), BF), vm((1024, 1024), BF), dma((4, 3, 2)), dma((4, 3, 2)),
            vm((512, 1024), F32), vm((512, 1024), BF), vm((512, 1024), BF), dma((4,)), dma((4,)),
            vm((2, 128, 512), BF), vm((2, 128, 512), BF), vm((2, 128, 512), BF),
            vm((2, 128, 512), BF), vm((2, 128, 512), BF), vm((2, 128, 512), BF), dma((3, 2)), dma((3, 2)),
            vm((1024, 1024), BF), dma((3, 2)), dma((3, 2)), dma((4, 2)), dma((4, 2)),
            vm((2, 512, 1024), BF), vm((4, 4, 8, 256), F32), dma((4, 4)), dma((4, 4)),
        ],
        compiler_params=pltpu.CompilerParams(
            collective_id=0, has_side_effects=True, vmem_limit_bytes=67043328
        ),
        name="muon_step",
    )(cotangent, activation)


def solution(mesh):
    return jax.shard_map(
        local,
        mesh=mesh,
        in_specs=(P("dp", None), P("dp", "mp")),
        out_specs=P("dp", "mp"),
        check_vma=False,
    )
```

time: 458 us -> 150 us (0.33)
  waiting for transfers between devices: 327 us -> 0 us
  Pallas kernels: 0 us -> 148 us
  blocking collectives: 64.3 us -> 0 us
  matrix products: 43.5 us -> 0 us
  between operations: 14.2 us -> 0.01 us
  other arithmetic: 6 us -> 0 us
    all_gather x4 -> x0, waiting for transfers between devices: 179 us -> none  [the longest x1 68.4 us: local(): weight_column = lax.all_gather(normalized, 'dp', axis=0, tiled=True)]
    pallas_call x0 -> x1, Pallas kernels: none -> 148 us  [local(): pl.pallas_call(kernel, out_shape=jax.ShapeDtypeStruct((256, 1024), BF), i...]
    reduce_scatter x2 -> x0, waiting for transfers between devices: 147 us -> none  [the longest x1 113 us: local(): lax.psum_scatter(lax.dot_general(section, activation, CONTRACT_FIRST, pre...]
    psum x1 -> x0, blocking collectives: 64.3 us -> none  [local(): sum_squares = lax.psum(jnp.sum(gradient * gradient), ('dp', 'mp'))]
    dot_general x4 -> x0, matrix products: 43.5 us -> none  [the longest x1 23.7 us: local(): lax.dot_general(section, activation, CONTRACT_FIRST, preferred_element_ty...]
  transfers between devices with their start and end apart: 6 -> 0, of which waited for: 6 -> 0; matrix products, arithmetic and copies ran while one was open for 0% -> 0% of each run, Pallas kernels for 0% -> 0%
where the time goes in v1:
time: 150 us
  Pallas kernels  148 us (99%)
  local copies, waits for them, and re-layouts  1.87 us (1%)
    pallas_call x1, Pallas kernels, local(): pl.pallas_call(kernel, out_shape=jax.ShapeDtypeStruct((256, 1024), BF), i...  148 us

profile of v1, /device:TPU:6, one launch (start us, length us, event | category | flops | bytes accessed | tf_op | source)
XLA Modules:
  0.0 149.7 jit_solution(17297751823404978590)
XLA Ops:
  0.0 147.8 %muon_step.1 = bf16[256,1024]{1,0:T(8,128)(2,1)} custom-call(bf16[2048,4096]{1,0:T(8,128)(2,1)} %c_ref.1, bf16[2048,1024]{1,0:T(8,128)(2,1)} %a_ref.1), custom_call_target="tpu_custom_call" | custom-call | tf_op jit(solution)/shard_map/muon_step/pallas_call | solution.py:477
  147.8 1.9 %copy.4 = bf16[256,1024]{1,0:T(8,128)(2,1)} copy(bf16[256,1024]{1,0:T(8,128)(2,1)} %muon_step.1) | data formatting | bytes 1048576

commit v2 on v1

--- a/solution.py
+++ b/solution.py
@@ -20,7 +20,8 @@
 F32 = jnp.float32
 NN = (((1,), (0,)), ((), ()))
 NT = (((1,), (1,)), ((), ()))
-SHIFT = (0, 1, 3, 2)
+FIRST_USE = ((2, 2), (2, 1), (1, 2), (2, 3), (3, 2), (2, 0), (0, 2), (1, 1), (3, 1), (1, 3), (3, 3), (1, 0), (3, 0), (0, 1), (0, 3), (0, 0))
+LATE = FIRST_USE[12:]
 PLUS, MINUS = 0, 1
 
 
@@ -30,11 +31,11 @@
 
 def kernel(
     c_ref, a_ref, out_ref,
-    a_t, a_in, c_in, a_sem, c_sem,
+    a_t, c_in, a_sem, c_sem,
     far_out, far_in, near_out, near_in, via_out, via_in, via_sum, own_sum, g_send, g_recv,
-    rs_far_out, rs_far_in, rs_near_out, rs_near_in, rs_via_out, rs_via_in, rs_via, rs_own, rs_send, rs_recv,
+    rs_far_out, rs_far_in, rs_near_out, rs_near_in, rs_via_out, rs_via_in, rs_send, rs_recv,
     grad, z_group, y_group, ag_send, ag_recv,
-    tile, half_out, half_in, pair_send, pair_recv,
+    half_in, pair_send, pair_recv,
     x_far_out, x_far_in, x_near_out, x_near_in, x_via_out, x_via_in, x_send, x_recv,
     gram, gx_send, gx_recv, gp_send, gp_recv,
     values, sq, sq_send, sq_recv,
@@ -67,36 +68,26 @@
         sent.append(c)
         return c
 
+    tile = via_sum.at[0:512]
+    half_out = a_t.at[0:512, 1024:2048]
+    rs_own = own_sum.at[:, 1]
+
     def load_a(q):
-        return pltpu.make_async_copy(a_ref.at[:, pl.ds(q * 256, 256)], a_in.at[q % 2], a_sem.at[q % 2])
+        slot = 4 * LATE[q][0] + LATE[q][1]
+        return pltpu.make_async_copy(a_ref.at[:, pl.ds(q * 256, 256)], c_in.at[slot], a_sem.at[q])
 
     def pick(k):
         return jnp.where(k == 0, 2, jnp.where(k == 1, 1, jnp.where(k == 2, 3, 0)))
 
-    def block(u):
-        first = u < 8
-        last = u >= 24
-        v = jnp.where(first, u, jnp.where(last, u - 24, u - 8))
-        pairs = first | last
-        k = jnp.where(pairs, v // 2, v // 4)
-        h = jnp.where(pairs, lax.rem(v, 2), lax.rem(v // 2, 2))
-        d = lax.rem(v, 2)
-        step = jnp.where(first, 2, jnp.where(last, 0, 1 + 2 * d))
-        one = jnp.where(h == 0, z, y)
-        two = jnp.where(h == 0, y, z)
-        one = lax.rem(one + step, 4)
-        two = lax.rem(two + pick(k), 4)
-        return jnp.where(h == 0, one * 4 + two, two * 4 + one)
-
-    def load_c(u):
-        slot = lax.rem(u, 4)
-        col = pl.multiple_of(block(u) * 256, 256)
+    def load_c(dz, dy):
+        slot = 4 * dz + dy
+        col = pl.multiple_of((4 * lax.rem(z + dz, 4) + lax.rem(y + dy, 4)) * 256, 256)
         return pltpu.make_async_copy(c_ref.at[:, pl.ds(col, 256)], c_in.at[slot], c_sem.at[slot])
 
-    load_a(0).start()
-    load_a(1).start()
-    for u in range(3):
-        load_c(jnp.int32(u)).start()
+    for q in range(4):
+        load_a(q).start()
+    for dz, dy in FIRST_USE[:12]:
+        load_c(dz, dy).start()
 
     barrier = pltpu.get_barrier_semaphore()
     for axis in ("z", "y", "x"):
@@ -106,21 +97,16 @@
 
     for q in range(4):
         load_a(q).wait()
-        a_t[pl.ds(q * 256, 256), :] = a_in[q % 2].T
-        if q < 2:
-            load_a(q + 2).start()
+        a_t[pl.ds(q * 256, 256), :] = c_in[4 * LATE[q][0] + LATE[q][1]].T
+        load_c(*LATE[q]).start()
     pl.semaphore_wait(barrier, 10)
 
     AXIS1 = ("z", "y")
     AXIS2 = ("y", "z")
 
-    def unit(h, u):
-        @pl.when(u + 3 < 32)
-        def _():
-            load_c(u + 3).start()
-
-        load_c(u).wait()
-        return dot(a_t[pl.ds(h * 512, 512), :], c_in[lax.rem(u, 4)])
+    def unit(h, step, k):
+        slot = 4 * step + pick(k) if h == 0 else 4 * pick(k) + step
+        return dot(a_t[pl.ds(h * 512, 512), :], c_in[slot])
 
     def far_copy(h, d, k):
         return copy(far_out.at[h, k, pl.ds(d * 256, 256)], far_in.at[h, d, k],
@@ -135,19 +121,34 @@
                     g_send.at[2, h, d, k], g_recv.at[2, h, d, k], AXIS1[h], d)
 
     def far_body(k, carry):
+        load_c(2, pick(k)).wait()
+
+        @pl.when(k > 0)
+        def _():
+            load_c(pick(k), 2).wait()
+
         for h in range(2):
-            far_out[h, k] = unit(h, 2 * k + h).astype(BF)
+            far_out[h, k] = unit(h, 2, k).astype(BF)
             for d in range(2):
                 far_copy(h, d, k).start()
         return carry
 
+    def piece(h, d, k):
+        return pl.ds((2 * h + d) * 256, 256), pl.ds(pl.multiple_of(k * 256, 256), 256)
+
     def near_body(k, carry):
+        for when, blocks in ((1, FIRST_USE[7:10]), (2, FIRST_USE[10:11]), (3, FIRST_USE[11:15])):
+            @pl.when(k == when)
+            def _():
+                for dz, dy in blocks:
+                    load_c(dz, dy).wait()
+
         for h in range(2):
             for d in range(2):
-                r = unit(h, 8 + 4 * k + 2 * h + d)
+                r = unit(h, 1 + 2 * d, k)
                 direct, relayed = 1 - d, d
                 near_out[h, d, k] = r[direct * 256:direct * 256 + 256].astype(BF)
-                via_sum[h, d, k] = r[relayed * 256:relayed * 256 + 256]
+                via_sum[piece(h, d, k)] = r[relayed * 256:relayed * 256 + 256]
                 near_copy(h, d, k).start()
         return carry
 
@@ -155,13 +156,17 @@
         for h in range(2):
             for d in range(2):
                 far_copy(h, d, k).wait_recv()
-                via_out[h, d, k] = (via_sum[h, d, k] + far_in[h, d, k].astype(F32)).astype(BF)
+                via_out[h, d, k] = (via_sum[piece(h, d, k)] + far_in[h, d, k].astype(F32)).astype(BF)
                 via_copy(h, d, k).start()
         return carry
 
     def own_body(k, carry):
+        @pl.when(k == 3)
+        def _():
+            load_c(0, 0).wait()
+
         for h in range(2):
-            own_sum[h, k] = unit(h, 24 + 2 * k + h)
+            own_sum[h, k] = unit(h, 0, k)
         return carry
 
     lax.fori_loop(0, 4, far_body, 0)
@@ -194,11 +199,11 @@
         elif slot == 1:
             rs_near_out[n, h, 0] = low.astype(BF)
             send(*rs_copy(n, h, 1, 0, axis))
-            rs_via[h, 0] = top
+            own_sum[h, 0, 0:256] = top
         elif slot == 2:
             rs_near_out[n, h, 1] = top.astype(BF)
             send(*rs_copy(n, h, 1, 1, axis))
-            rs_via[h, 1] = low
+            own_sum[h, 0, 256:512] = low
         else:
             rs_own[h, 0:256] = top
             rs_own[h, 256:512] = low
@@ -206,7 +211,7 @@
     def rs_relay(n, h, axis):
         for d in range(2):
             copy(*rs_copy(n, h, 0, d, axis)).wait_recv()
-            rs_via_out[n, h, d] = (rs_via[h, d] + rs_far_in[n, h, d].astype(F32)).astype(BF)
+            rs_via_out[n, h, d] = (own_sum[h, 0, d * 256:d * 256 + 256] + rs_far_in[n, h, d].astype(F32)).astype(BF)
             send(*rs_copy(n, h, 2, d, axis))
 
     def rs_finish(n, h, axis):
@@ -480,19 +485,18 @@
         in_specs=[pl.BlockSpec(memory_space=pl.ANY)] * 2,
         out_specs=pl.BlockSpec(memory_space=pltpu.VMEM),
         scratch_shapes=[
-            vm((1024, 2048), BF), vm((2, 2048, 256), BF), vm((4, 2048, 256), BF), dma((2,)), dma((4,)),
+            vm((1024, 2048), BF), vm((16, 2048, 256), BF), dma((4,)), dma((16,)),
             vm((2, 4, 512, 256), BF), vm((2, 2, 4) + piece, BF),
             vm((2, 2, 4) + piece, BF), vm((2, 2, 4) + piece, BF),
             vm((2, 2, 4) + piece, BF), vm((2, 2, 4) + piece, BF),
-            vm((2, 2, 4) + piece, F32), vm((2, 4, 512, 256), F32),
+            vm((1024, 1024), F32), vm((2, 4, 512, 256), F32),
             dma((3, 2, 2, 4)), dma((3, 2, 2, 4)),
             vm((3, 2, 512, 256), BF), vm((3, 2, 2) + piece, BF),
             vm((3, 2, 2) + piece, BF), vm((3, 2, 2) + piece, BF),
             vm((3, 2, 2) + piece, BF), vm((3, 2, 2) + piece, BF),
-            vm((2, 2) + piece, F32), vm((2, 512, 256), F32),
             dma((3, 2, 3, 2)), dma((3, 2, 3, 2)),
             vm((2, 512, 256), F32), vm((1024, 1024), BF), vm((1024, 1024), BF), dma((4, 3, 2)), dma((4, 3, 2)),
-            vm((512, 1024), F32), vm((512, 1024), BF), vm((512, 1024), BF), dma((4,)), dma((4,)),
+            vm((512, 1024), BF), dma((4,)), dma((4,)),
             vm((2, 128, 512), BF), vm((2, 128, 512), BF), vm((2, 128, 512), BF),
             vm((2, 128, 512), BF), vm((2, 128, 512), BF), vm((2, 128, 512), BF), dma((3, 2)), dma((3, 2)),
             vm((1024, 1024), BF), dma((3, 2)), dma((3, 2)), dma((4, 2)), dma((4, 2)),

time: 150 us -> 148 us (0.987)
  Pallas kernels: 148 us -> 146 us
    pallas_call x1, Pallas kernels: 148 us -> 146 us  [local(): pl.pallas_call(kernel, out_shape=jax.ShapeDtypeStruct((256, 1024), BF), i...]
where the time goes in v2:
time: 148 us
  Pallas kernels  146 us (99%)
  local copies, waits for them, and re-layouts  1.87 us (1%)
    pallas_call x1, Pallas kernels, local(): pl.pallas_call(kernel, out_shape=jax.ShapeDtypeStruct((256, 1024), BF), i...  146 us

profile of v2, /device:TPU:6, one launch (start us, length us, event | category | flops | bytes accessed | tf_op | source)
XLA Modules:
  0.0 148.1 jit_solution(10833619207605654213)
XLA Ops:
  0.0 146.2 %muon_step.1 = bf16[256,1024]{1,0:T(8,128)(2,1)} custom-call(bf16[2048,4096]{1,0:T(8,128)(2,1)} %c_ref.1, bf16[2048,1024]{1,0:T(8,128)(2,1)} %a_ref.1), custom_call_target="tpu_custom_call" | custom-call | tf_op jit(solution)/shard_map/muon_step/pallas_call | solution.py:482
  146.2 1.9 %copy.4 = bf16[256,1024]{1,0:T(8,128)(2,1)} copy(bf16[256,1024]{1,0:T(8,128)(2,1)} %muon_step.1) | data formatting | bytes 1048576

commit v3 on v2

--- a/solution.py
+++ b/solution.py
@@ -136,6 +136,14 @@
     def piece(h, d, k):
         return pl.ds((2 * h + d) * 256, 256), pl.ds(pl.multiple_of(k * 256, 256), 256)
 
+    def via_body(k, carry):
+        for h in range(2):
+            for d in range(2):
+                far_copy(h, d, k).wait_recv()
+                via_out[h, d, k] = (via_sum[piece(h, d, k)] + far_in[h, d, k].astype(F32)).astype(BF)
+                via_copy(h, d, k).start()
+        return carry
+
     def near_body(k, carry):
         for when, blocks in ((1, FIRST_USE[7:10]), (2, FIRST_USE[10:11]), (3, FIRST_USE[11:15])):
             @pl.when(k == when)
@@ -150,15 +158,7 @@
                 near_out[h, d, k] = r[direct * 256:direct * 256 + 256].astype(BF)
                 via_sum[piece(h, d, k)] = r[relayed * 256:relayed * 256 + 256]
                 near_copy(h, d, k).start()
-        return carry
-
-    def via_body(k, carry):
-        for h in range(2):
-            for d in range(2):
-                far_copy(h, d, k).wait_recv()
-                via_out[h, d, k] = (via_sum[piece(h, d, k)] + far_in[h, d, k].astype(F32)).astype(BF)
-                via_copy(h, d, k).start()
-        return carry
+        return via_body(k, carry)
 
     def own_body(k, carry):
         @pl.when(k == 3)
@@ -171,7 +171,6 @@
 
     lax.fori_loop(0, 4, far_body, 0)
     lax.fori_loop(0, 4, near_body, 0)
-    lax.fori_loop(0, 4, via_body, 0)
     lax.fori_loop(0, 4, own_body, 0)
 
     def first_sum(h, k):

time: 148 us -> 143 us (0.966)
  Pallas kernels: 146 us -> 140 us
    pallas_call x1, Pallas kernels: 146 us -> 140 us  [local(): pl.pallas_call(kernel, out_shape=jax.ShapeDtypeStruct((256, 1024), BF), i...]
where the time goes in v3:
time: 143 us; the launch traced here: 142 us
  Pallas kernels  140 us (98%)
  local copies, waits for them, and re-layouts  1.87 us (1%)
    pallas_call x1, Pallas kernels, local(): pl.pallas_call(kernel, out_shape=jax.ShapeDtypeStruct((256, 1024), BF), i...  140 us

profile of v3, /device:TPU:6, one launch (start us, length us, event | category | flops | bytes accessed | tf_op | source)
XLA Modules:
  0.0 142.4 jit_solution(13642083635875359789)
XLA Ops:
  0.0 140.5 %muon_step.1 = bf16[256,1024]{1,0:T(8,128)(2,1)} custom-call(bf16[2048,4096]{1,0:T(8,128)(2,1)} %c_ref.1, bf16[2048,1024]{1,0:T(8,128)(2,1)} %a_ref.1), custom_call_target="tpu_custom_call" | custom-call | tf_op jit(solution)/shard_map/muon_step/pallas_call | solution.py:481
  140.5 1.9 %copy.4 = bf16[256,1024]{1,0:T(8,128)(2,1)} copy(bf16[256,1024]{1,0:T(8,128)(2,1)} %muon_step.1) | data formatting | bytes 1048576

commit v4 on v3

--- a/solution.py
+++ b/solution.py
@@ -171,7 +171,6 @@
 
     lax.fori_loop(0, 4, far_body, 0)
     lax.fori_loop(0, 4, near_body, 0)
-    lax.fori_loop(0, 4, own_body, 0)
 
     def first_sum(h, k):
         for d in range(2):
@@ -247,9 +246,11 @@
             copy(*ag_copy(n, buf, rows, 2, d, axis)).wait_recv()
 
     for k, slot in ((0, 3), (1, 1), (2, 2)):
+        own_body(jnp.int32(k), 0)
         for h in range(2):
             top, low = first_sum(h, k)
             rs_put(0, h, AXIS2[h], slot, top, low)
+    own_body(jnp.int32(3), 0)
     for h in range(2):
         rs_relay(0, h, AXIS2[h])
     for h in range(2):

time: 143 us -> 143 us (level)
  no operation moved by 1% of the time
where the time goes in v4:
time: 143 us; the launch traced here: 142 us
  Pallas kernels  140 us (98%)
  local copies, waits for them, and re-layouts  1.87 us (1%)
    pallas_call x1, Pallas kernels, local(): pl.pallas_call(kernel, out_shape=jax.ShapeDtypeStruct((256, 1024), BF), i...  140 us

profile of v4, /device:TPU:6, one launch (start us, length us, event | category | flops | bytes accessed | tf_op | source)
XLA Modules:
  0.0 142.4 jit_solution(14355581746612435028)
XLA Ops:
  0.0 140.5 %muon_step.1 = bf16[256,1024]{1,0:T(8,128)(2,1)} custom-call(bf16[2048,4096]{1,0:T(8,128)(2,1)} %c_ref.1, bf16[2048,1024]{1,0:T(8,128)(2,1)} %a_ref.1), custom_call_target="tpu_custom_call" | custom-call | tf_op jit(solution)/shard_map/muon_step/pallas_call | solution.py:482
  140.5 1.9 %copy.4 = bf16[256,1024]{1,0:T(8,128)(2,1)} copy(bf16[256,1024]{1,0:T(8,128)(2,1)} %muon_step.1) | data formatting | bytes 1048576
